TPU v7x, 256 devices: a whole 4x4x8 slice. The times are simulated.
256 devices in a mesh: ckpt: 16 (over z, core), rows: 16 (over y, x).
Axes of the slice: x: 4, y: 4, z: 8, core: 2. Of those that a mesh axis runs over, the one named last changes fastest.
Arguments:
- deltas: bfloat16 [16, 4096, 14336], P('ckpt', 'rows'), may hold values from -24 to 24
- start_basis: bfloat16 [16, 14336, 64], P('ckpt', 'rows'), may hold values from -6 to 6
- edit_order: int32 [16], replicated, may hold values from 0 to 15, each once
Outputs:
- merged: bfloat16 [4096, 14336], P('rows', 'ckpt')
Inputs may be any that keep to these rules, and one draw needn't show every extreme that they name: `edit_order`: a permutation: each of 0 to 15 appears once.
All inputs are finite; a program needn't handle non-finite values.
Results may differ from a plain program's by a relative error of at most 0.034.
Values may be sent and summed in bfloat16 or wider, within the bound.
A program may use at most 64 MiB of HBM per device.

v0:
```python
import math
import jax
import jax.numpy as jnp
from jax import lax
from jax.sharding import PartitionSpec as P

RANK = 64
SUB_ITERS = 2
NS_ITERS = 4


def broadcast(value, axis, source):
    kept = jnp.where(lax.axis_index(axis) == source, value, 0).astype(value.dtype)
    return lax.psum(kept, axis)


def solve_right(raw, lower_factor):
    return lax.linalg.triangular_solve(
        lower_factor, raw, left_side=False, lower=True, transpose_a=True
    ).astype(jnp.bfloat16)


def local_gram(raw):
    return jnp.dot(raw.T, raw, precision=lax.Precision.HIGHEST)


def cross_gram(stacked, own_cols):
    return lax.dot_general(
        stacked, own_cols, (((0,), (0,)), ((), ())), preferred_element_type=jnp.float32
    )


def update_cols(own_cols, stacked, gram_cols, lead_factor, tail_factor):
    product = jnp.dot(stacked.astype(jnp.float32), gram_cols, precision=lax.Precision.HIGHEST)
    return (lead_factor * own_cols.astype(jnp.float32) + tail_factor * product).astype(jnp.bfloat16)


def body(deltas, start_basis, edit_order):
    changes = deltas[0]
    basis_now = start_basis[0]
    local_rows = changes.shape[0]
    left_basis = jnp.zeros((local_rows, RANK), jnp.bfloat16)
    lower_factor = jnp.zeros((RANK, RANK), jnp.float32)
    for sweep in range(SUB_ITERS):
        left_raw = jnp.dot(
            changes,
            lax.all_gather(basis_now, "rows", axis=0, tiled=True),
            preferred_element_type=jnp.float32,
        )
        left_gram = lax.psum(local_gram(left_raw), "rows")
        left_basis = solve_right(left_raw, jnp.linalg.cholesky(left_gram))
        right_raw = lax.psum_scatter(
            lax.dot_general(
                changes, left_basis, (((0,), (0,)), ((), ())), preferred_element_type=jnp.float32
            ).astype(jnp.bfloat16),
            "rows",
            scatter_dimension=0,
            tiled=True,
        ).astype(jnp.float32)
        right_gram = lax.psum(local_gram(right_raw), "rows")
        lower_factor = jnp.linalg.cholesky(right_gram)
        basis_now = solve_right(right_raw, lower_factor)
    ckpt_count = lax.axis_size("ckpt")
    rows_count = lax.axis_size("rows")
    ckpt_index = lax.axis_index("ckpt")
    left_now = left_basis
    right_now = basis_now
    for step in range(NS_ITERS):
        left_all, right_all = (
            lax.all_gather(left_now, "ckpt", axis=1, tiled=True),
            lax.all_gather(right_now, "ckpt", axis=1, tiled=True),
        )
        gram_left = cross_gram(left_all, left_now)
        gram_right = cross_gram(right_all, right_now)
        gram_left, gram_right = (
            lax.psum(gram_left.astype(jnp.bfloat16), "rows").astype(jnp.float32),
            lax.psum(gram_right.astype(jnp.bfloat16), "rows").astype(jnp.float32),
        )
        if step == 0:
            lead_factor = 1.5 / math.sqrt(ckpt_count)
            tail_factor = -0.5 / (ckpt_count * math.sqrt(ckpt_count))
        else:
            lead_factor = 1.5
            tail_factor = -0.5
        left_now = update_cols(left_now, left_all, gram_left, lead_factor, tail_factor)
        right_now = update_cols(right_now, right_all, gram_right, lead_factor, tail_factor)
    position = jnp.sum(jnp.where(jnp.arange(ckpt_count) == ckpt_index, edit_order, 0))
    weight_now = (1 + position).astype(jnp.float32) / ckpt_count
    scaled_left = jnp.dot(
        left_now.astype(jnp.float32), lower_factor * weight_now, precision=lax.Precision.HIGHEST
    ).astype(jnp.bfloat16)
    left_stack, right_block = (
        lax.all_gather(scaled_left, "ckpt", axis=1, tiled=True),
        lax.all_gather(right_now, "ckpt", axis=1, tiled=True),
    )
    holder = ckpt_index * rows_count // ckpt_count
    right_held = broadcast(right_block, "rows", holder)
    merged = lax.dot_general(
        left_stack, right_held, (((1,), (1,)), ((), ())), preferred_element_type=jnp.float32
    )
    return merged.astype(jnp.bfloat16)


def solution(mesh):
    return jax.shard_map(
        body,
        mesh=mesh,
        in_specs=(P("ckpt", "rows", None), P("ckpt", "rows", None), P()),
        out_specs=P("rows", "ckpt"),
        check_vma=False,
    )
```

profile of v0, /device:TPU:1, one launch (start us, length us, event | category | flops | bytes accessed | tf_op | source)
XLA Modules:
  0.0 1361.7 jit_solution(2458196330878033833)
XLA Ops:
  7.3 54.2 %all-gather.21.cloned.1.call-done = bf16[1,14336,64]{1,2,0:T(8,128)(2,1)} async-done(((bf16[1,896,64]{1,2,0:T(8,128)(2,1)}), bf16[1,14336,64]{1,2,0:T(8,128)(2,1)}) %all-gather.21.cloned.1.call-update) | async-done | bytes 1835024 | tf_op jit(solution)/shard_map/all_gather | solution.py:47
  61.5 5.9 fusion.6
  67.6 58.2 %psum.91 = f32[64,64]{0,1:T(8,128)S(1)} all-reduce(f32[64,64]{0,1:T(8,128)S(1)} %fusion.55), channel_id=1, replica_groups=mesh['ckpt'=16,'rows'=16] {'rows'}, use_global_device_ids=true, to_apply=%region_0.0 | all-reduce | flops 4096 | bytes 32768 | tf_op jit(solution)/shard_map/psum | solution.py:50
  125.9 5.8 cholesky.74
  133.1 4.9 custom-call.10
  145.8 92.6 %reduce-scatter.7.cloned.1.call-done = bf16[896,64]{1,0:T(8,128)(2,1)} async-done(((bf16[14336,64]{1,0:T(8,128)(2,1)}), bf16[896,64]{1,0:T(8,128)(2,1)}) %reduce-scatter.7.cloned.1.call-update) | async-done | bytes 114704
  239.6 57.9 %psum.92 = f32[64,64]{0,1:T(8,128)S(1)} all-reduce(f32[64,64]{0,1:T(8,128)S(1)} %fusion.56), channel_id=1, replica_groups=mesh['ckpt'=16,'rows'=16] {'rows'}, use_global_device_ids=true, to_apply=%region_4.7 | all-reduce | flops 4096 | bytes 32768 | tf_op jit(solution)/shard_map/psum | solution.py:60
  297.6 5.8 cholesky.85
  311.9 60.3 %all-gather.9.cloned.1.call-done = bf16[14336,64]{0,1:T(8,128)(2,1)} async-done(((bf16[896,64]{0,1:T(8,128)(2,1)}), bf16[14336,64]{0,1:T(8,128)(2,1)}) %all-gather.9.cloned.1.call-update) | async-done | bytes 1835024 | tf_op jit(solution)/shard_map/all_gather | solution.py:47
  372.1 6.0 fusion.3
  378.3 58.2 %psum.93 = f32[64,64]{0,1:T(8,128)S(1)} all-reduce(f32[64,64]{0,1:T(8,128)S(1)} %fusion.57), channel_id=1, replica_groups=mesh['ckpt'=16,'rows'=16] {'rows'}, use_global_device_ids=true, to_apply=%region_5.9 | all-reduce | flops 4096 | bytes 32768 | tf_op jit(solution)/shard_map/psum | solution.py:50
  436.6 5.8 cholesky.96
  443.8 4.9 custom-call.12
  456.5 92.5 %reduce-scatter.9.cloned.1.call-done = bf16[896,64]{1,0:T(8,128)(2,1)} async-done(((bf16[14336,64]{1,0:T(8,128)(2,1)}), bf16[896,64]{1,0:T(8,128)(2,1)}) %reduce-scatter.9.cloned.1.call-update) | async-done | bytes 114704
  550.3 57.9 %psum.98 = f32[64,64]{0,1:T(8,128)S(1)} all-reduce(f32[64,64]{0,1:T(8,128)S(1)} %fusion.58), channel_id=1, replica_groups=mesh['ckpt'=16,'rows'=16] {'rows'}, use_global_device_ids=true, to_apply=%region_11.15 | all-reduce | flops 4096 | bytes 32768 | tf_op jit(solution)/shard_map/psum | solution.py:60
  608.2 5.8 cholesky.107
  615.4 4.9 custom-call.13
  622.5 52.0 %all-gather.11.cloned.1.call-done = bf16[896,1024]{0,1:T(8,128)(2,1)} async-done(((bf16[896,64]{0,1:T(8,128)(2,1)}), bf16[896,1024]{0,1:T(8,128)(2,1)}) %all-gather.11.cloned.1.call-update) | async-done | bytes 1835024 | tf_op jit(solution)/shard_map/all_gather | solution.py:71
  677.6 91.3 %all-reduce.10.cloned.1.call-done = bf16[1024,64]{1,0:T(8,128)(2,1)} async-done(((bf16[1024,64]{1,0:T(8,128)(2,1)}), bf16[1024,64]{1,0:T(8,128)(2,1)}) %all-reduce.10.cloned.1.call-update) | async-done | bytes 131088 | tf_op jit(solution)/shard_map/psum | solution.py:77
  771.0 21.6 %all_gather.38 = bf16[256,1024]{0,1:T(8,128)(2,1)S(1)} all-gather(bf16[256,64]{0,1:T(8,128)(2,1)S(1)} %fusion.24), channel_id=1, replica_groups=mesh['ckpt'=16,'rows'=16] {'ckpt'}, dimensions={1}, use_global_device_ids=true | all-gather | bytes 557056 | tf_op jit(solution)/shard_map/all_gather | solution.py:70
  793.6 18.5 %all-gather.13.cloned.1.call-done = bf16[896,1024]{0,1:T(8,128)(2,1)} async-done(((bf16[896,64]{0,1:T(8,128)(2,1)}), bf16[896,1024]{0,1:T(8,128)(2,1)}) %all-gather.13.cloned.1.call-update) | async-done | bytes 1835024 | tf_op jit(solution)/shard_map/all_gather | solution.py:71
  815.1 92.2 %all-reduce.18.cloned.1.call-done = (bf16[1024,64]{1,0:T(8,128)(2,1)}, bf16[1024,64]{1,0:T(8,128)(2,1)}) async-done(((bf16[1024,64]{1,0:T(8,128)(2,1)}, bf16[1024,64]{1,0:T(8,128)(2,1)}), (bf16[1024,64]{1,0:T(8,128)(2,1)}, bf16[1024,64]{1,0:T(8,128)(2,1)})) %all-reduce.18.cloned.1.call-update) | async-done | bytes 262160 | tf_op jit(solution)/shard_map/psum | solution.py:76
  909.8 21.6 %all_gather.39 = bf16[256,1024]{0,1:T(8,128)(2,1)S(1)} all-gather(bf16[256,64]{0,1:T(8,128)(2,1)S(1)} %fusion.25), channel_id=1, replica_groups=mesh['ckpt'=16,'rows'=16] {'ckpt'}, dimensions={1}, use_global_device_ids=true | all-gather | bytes 557056 | tf_op jit(solution)/shard_map/all_gather | solution.py:70
  932.4 18.3 %all-gather.15.cloned.1.call-done = bf16[896,1024]{0,1:T(8,128)(2,1)} async-done(((bf16[896,64]{0,1:T(8,128)(2,1)}), bf16[896,1024]{0,1:T(8,128)(2,1)}) %all-gather.15.cloned.1.call-update) | async-done | bytes 1835024 | tf_op jit(solution)/shard_map/all_gather | solution.py:71
  953.8 92.2 %all-reduce.16.cloned.1.call-done = (bf16[1024,64]{1,0:T(8,128)(2,1)}, bf16[1024,64]{1,0:T(8,128)(2,1)}) async-done(((bf16[1024,64]{1,0:T(8,128)(2,1)}, bf16[1024,64]{1,0:T(8,128)(2,1)}), (bf16[1024,64]{1,0:T(8,128)(2,1)}, bf16[1024,64]{1,0:T(8,128)(2,1)})) %all-reduce.16.cloned.1.call-update) | async-done | bytes 262160 | tf_op jit(solution)/shard_map/psum | solution.py:76
  1048.4 21.6 %all_gather.40 = bf16[256,1024]{0,1:T(8,128)(2,1)S(1)} all-gather(bf16[256,64]{0,1:T(8,128)(2,1)S(1)} %fusion.26), channel_id=1, replica_groups=mesh['ckpt'=16,'rows'=16] {'ckpt'}, dimensions={1}, use_global_device_ids=true | all-gather | bytes 557056 | tf_op jit(solution)/shard_map/all_gather | solution.py:70
  1071.0 18.4 %all-gather.17.cloned.1.call-done = bf16[896,1024]{0,1:T(8,128)(2,1)} async-done(((bf16[896,64]{0,1:T(8,128)(2,1)}), bf16[896,1024]{0,1:T(8,128)(2,1)}) %all-gather.17.cloned.1.call-update) | async-done | bytes 1835024 | tf_op jit(solution)/shard_map/all_gather | solution.py:71
  1092.4 92.1 %all-reduce.14.cloned.1.call-done = (bf16[1024,64]{1,0:T(8,128)(2,1)}, bf16[1024,64]{1,0:T(8,128)(2,1)}) async-done(((bf16[1024,64]{1,0:T(8,128)(2,1)}, bf16[1024,64]{1,0:T(8,128)(2,1)}), (bf16[1024,64]{1,0:T(8,128)(2,1)}, bf16[1024,64]{1,0:T(8,128)(2,1)})) %all-reduce.14.cloned.1.call-update) | async-done | bytes 262160 | tf_op jit(solution)/shard_map/psum | solution.py:76
  1187.0 21.6 %all_gather.41 = bf16[256,1024]{0,1:T(8,128)(2,1)S(1)} all-gather(bf16[256,64]{0,1:T(8,128)(2,1)S(1)} %fusion.27), channel_id=1, replica_groups=mesh['ckpt'=16,'rows'=16] {'ckpt'}, dimensions={1}, use_global_device_ids=true | all-gather | bytes 557056 | tf_op jit(solution)/shard_map/all_gather | solution.py:70
  1209.6 18.3 %all-gather.19.cloned.1.call-done = bf16[896,1024]{0,1:T(8,128)(2,1)} async-done(((bf16[896,64]{0,1:T(8,128)(2,1)}), bf16[896,1024]{0,1:T(8,128)(2,1)}) %all-gather.19.cloned.1.call-update) | async-done | bytes 1835024 | tf_op jit(solution)/shard_map/all_gather | solution.py:94
  1231.2 98.1 %all-reduce.12.cloned.1.call-done = (bf16[1024,64]{1,0:T(8,128)(2,1)}, bf16[896,1024]{0,1:T(8,128)(2,1)}) async-done(((bf16[1024,64]{1,0:T(8,128)(2,1)}, bf16[896,1024]{0,1:T(8,128)(2,1)}), (bf16[1024,64]{1,0:T(8,128)(2,1)}, bf16[896,1024]{0,1:T(8,128)(2,1)})) %all-reduce.12.cloned.1.call-update) | async-done | bytes 1966096 | tf_op jit(solution)/shard_map/psum | solution.py:76
  1331.3 20.8 %all_gather.42 = bf16[256,1024]{0,1:T(8,128)(2,1)S(1)} all-gather(bf16[256,64]{0,1:T(8,128)(2,1)S(1)} %convolution_convert_fusion.11), channel_id=1, replica_groups=mesh['ckpt'=16,'rows'=16] {'ckpt'}, dimensions={1}, use_global_device_ids=true | all-gather | bytes 557056 | tf_op jit(solution)/shard_map/all_gather | solution.py:93
  (107 shorter events, 67.2 us)
Async XLA Ops:
  6.5 54.9 %all-gather.21.cloned.1.call-start = ((), (), s32[]{:S(2)}) async-start(), calls=%async_computation.9 | async-start | bytes 1949696 | tf_op jit(solution)/shard_map/all_gather | solution.py:47
  7.3 231.1 %reduce-scatter.7.cloned.1.call-start = ((), (), s32[]{:S(2)}) async-start(), calls=%async_computation.10 | async-start | bytes 3899392
  145.7 226.4 %all-gather.9.cloned.1.call-start = ((), (), s32[]{:S(2)}) async-start(), calls=%async_computation.2 | async-start | bytes 1949696 | tf_op jit(solution)/shard_map/all_gather | solution.py:47
  311.8 237.2 %reduce-scatter.9.cloned.1.call-start = ((), (), s32[]{:S(2)}) async-start(), calls=%async_computation.11 | async-start | bytes 3899392
  456.4 218.2 %all-gather.11.cloned.1.call-start = ((), (), s32[]{:S(2)}) async-start(), calls=%async_computation.3 | async-start | bytes 1949696 | tf_op jit(solution)/shard_map/all_gather | solution.py:71
  622.5 146.4 %copy-start.7 = (bf16[896,64]{0,1:T(8,128)(2,1)S(1)}, bf16[896,64]{0,1:T(8,128)(2,1)}, u32[]{:S(2)}) copy-start(bf16[896,64]{0,1:T(8,128)(2,1)} %fusion.18) | copy-start | bytes 344068
  622.5 146.4 %all-reduce.10.cloned.1.call-start = ((), (), s32[]{:S(2)}) async-start(), calls=%async_computation.4 | async-start | bytes 524288 | tf_op jit(solution)/shard_map/psum | solution.py:77
  674.6 94.3 %copy-start.3 = (bf16[896,1024]{0,1:T(8,128)(2,1)S(1)}, bf16[896,1024]{0,1:T(8,128)(2,1)}, u32[]{:S(2)}) copy-start(bf16[896,1024]{0,1:T(8,128)(2,1)} %all-gather.11.cloned.1.call-done) | copy-start | bytes 5505028
  677.6 134.5 %all-gather.13.cloned.1.call-start = ((), (), s32[]{:S(2)}) async-start(), calls=%async_computation.5 | async-start | bytes 1949696 | tf_op jit(solution)/shard_map/all_gather | solution.py:71
  771.0 136.4 %all-reduce.18.cloned.1.call-start = ((), (), s32[]{:S(2)}) async-start(), calls=%async_computation.15 | async-start | bytes 1048576 | tf_op jit(solution)/shard_map/psum | solution.py:76
  792.6 114.7 %copy-start.6 = (bf16[896,64]{0,1:T(8,128)(2,1)S(1)}, bf16[896,64]{0,1:T(8,128)(2,1)}, u32[]{:S(2)}) copy-start(bf16[896,64]{0,1:T(8,128)(2,1)} %fusion.13) | copy-start | bytes 344068
  812.1 95.3 %copy-start.2 = (bf16[896,1024]{0,1:T(8,128)(2,1)S(1)}, bf16[896,1024]{0,1:T(8,128)(2,1)}, u32[]{:S(2)}) copy-start(bf16[896,1024]{0,1:T(8,128)(2,1)} %all-gather.13.cloned.1.call-done) | copy-start | bytes 5505028
  815.1 135.7 %all-gather.15.cloned.1.call-start = ((), (), s32[]{:S(2)}) async-start(), calls=%async_computation.6 | async-start | bytes 1949696 | tf_op jit(solution)/shard_map/all_gather | solution.py:71
  907.4 2.2 copy-start.9
  909.4 41.3 %copy-start.4 = (bf16[896,64]{0,1:T(8,128)(2,1)S(1)}, bf16[896,64]{0,1:T(8,128)(2,1)}, u32[]{:S(2)}) copy-start(bf16[896,64]{0,1:T(8,128)(2,1)} %fusion.14) | copy-start | bytes 344068
  909.5 136.5 %all-reduce.16.cloned.1.call-start = ((), (), s32[]{:S(2)}) async-start(), calls=%async_computation.14 | async-start | bytes 1048576 | tf_op jit(solution)/shard_map/psum | solution.py:76
  950.7 95.3 %copy-start = (bf16[896,1024]{0,1:T(8,128)(2,1)S(1)}, bf16[896,1024]{0,1:T(8,128)(2,1)}, u32[]{:S(2)}) copy-start(bf16[896,1024]{0,1:T(8,128)(2,1)} %all-gather.15.cloned.1.call-done) | copy-start | bytes 5505028
  953.7 135.6 %all-gather.17.cloned.1.call-start = ((), (), s32[]{:S(2)}) async-start(), calls=%async_computation.7 | async-start | bytes 1949696 | tf_op jit(solution)/shard_map/all_gather | solution.py:71
  1046.0 2.2 copy-start.10
  1048.1 41.3 %copy-start.5 = (bf16[896,64]{0,1:T(8,128)(2,1)S(1)}, bf16[896,64]{0,1:T(8,128)(2,1)}, u32[]{:S(2)}) copy-start(bf16[896,64]{0,1:T(8,128)(2,1)} %fusion.15) | copy-start | bytes 344068
  1048.1 136.5 %all-reduce.14.cloned.1.call-start = ((), (), s32[]{:S(2)}) async-start(), calls=%async_computation.13 | async-start | bytes 1048576 | tf_op jit(solution)/shard_map/psum | solution.py:76
  1089.3 95.2 %copy-start.1 = (bf16[896,1024]{0,1:T(8,128)(2,1)S(1)}, bf16[896,1024]{0,1:T(8,128)(2,1)}, u32[]{:S(2)}) copy-start(bf16[896,1024]{0,1:T(8,128)(2,1)} %all-gather.17.cloned.1.call-done) | copy-start | bytes 5505028
  1092.3 135.6 %all-gather.19.cloned.1.call-start = ((), (), s32[]{:S(2)}) async-start(), calls=%async_computation.8 | async-start | bytes 1949696 | tf_op jit(solution)/shard_map/all_gather | solution.py:94
  1184.5 2.2 copy-start.8
  1186.6 142.7 %all-reduce.12.cloned.1.call-start = ((), (), s32[]{:S(2)}) async-start(), calls=%async_computation.12 | async-start | bytes 4194304 | tf_op jit(solution)/shard_map/psum | solution.py:76
  1229.3 0.7 copy-start.11
Sparse Core Ops, SparseCore 0:
  9.8 51.6 all-gather.20
  145.8 92.4 reduce-scatter.6
  311.9 60.1 all-gather.8
  456.5 92.4 reduce-scatter.8
  622.6 51.9 all-gather.10
  677.7 91.1 all-reduce.9
  771.1 40.9 all-gather.12
  815.3 92.0 all-reduce.17
  909.6 41.0 all-gather.14
  953.8 92.0 all-reduce.15
  1048.2 41.0 all-gather.16
  1092.5 92.0 all-reduce.13
  1186.8 41.1 all-gather.18
  1231.1 98.1 all-reduce.11
where the time goes:
time: 1360 us
  waiting for transfers between devices  892 us (66%)
  blocking collectives  339 us (25%)
  matrix products  56.3 us (4%)
  other arithmetic  50.3 us (4%)
  between operations  14.1 us (1%)
    psum x4, waiting for transfers between devices, body(): lax.psum(gram_left.astype(jnp.bfloat16), 'rows').astype(jnp.float32)  375 us
    unnamed x16, waiting for transfers between devices  186 us
    all_gather x5, waiting for transfers between devices, body(): lax.all_gather(right_now, 'ckpt', axis=1, tiled=True)  126 us
    psum x2, blocking collectives, body(): left_gram = lax.psum(local_gram(left_raw), 'rows')  116 us
    psum x2, blocking collectives, body(): right_gram = lax.psum(local_gram(right_raw), 'rows')  116 us
    all_gather x2, waiting for transfers between devices, body(): lax.all_gather(basis_now, 'rows', axis=0, tiled=True)  114 us
    psum x1, waiting for transfers between devices, body(): lax.psum(gram_right.astype(jnp.bfloat16), 'rows').astype(jnp.float32)  91.3 us
    all_gather x4, blocking collectives, body(): lax.all_gather(left_now, 'ckpt', axis=1, tiled=True)  86.5 us
  transfers between devices with their start and end apart: 14, of which 14 were waited for; matrix products, arithmetic and copies ran while one was open for 0% of the time, Pallas kernels for 0%

commit v1 on v0

--- a/solution.py
+++ b/solution.py
@@ -47,7 +47,8 @@
             lax.all_gather(basis_now, "rows", axis=0, tiled=True),
             preferred_element_type=jnp.float32,
         )
-        left_gram = lax.psum(local_gram(left_raw), "rows")
+        compute_the_trees = lambda mat: jnp.sum(jax.lax.all_gather(mat, "rows"), axis=0)
+        left_gram = compute_the_trees(local_gram(left_raw))
         left_basis = solve_right(left_raw, jnp.linalg.cholesky(left_gram))
         right_raw = lax.psum_scatter(
             lax.dot_general(

time: 1360 us -> 1270 us (0.934)
  blocking collectives: 339 us -> 259 us
    psum x2 -> x0, blocking collectives: 116 us -> none  [body(): left_gram = lax.psum(local_gram(left_raw), 'rows')]
    all_gather x0 -> x2, blocking collectives: none -> 35.8 us  [body(): jax.lax.all_gather(mat, 'rows')]
where the time goes in v1:
time: 1270 us
  waiting for transfers between devices  879 us (69%)
  blocking collectives  259 us (20%)
  matrix products  56.3 us (4%)
  other arithmetic  50.4 us (4%)
  between operations  14.1 us (1%)
    psum x4, waiting for transfers between devices, body(): lax.psum(gram_left.astype(jnp.bfloat16), 'rows').astype(jnp.float32)  375 us
    unnamed x16, waiting for transfers between devices  174 us
    all_gather x5, waiting for transfers between devices, body(): lax.all_gather(right_now, 'ckpt', axis=1, tiled=True)  126 us
    psum x2, blocking collectives, body(): right_gram = lax.psum(local_gram(right_raw), 'rows')  116 us
    all_gather x2, waiting for transfers between devices, body(): lax.all_gather(basis_now, 'rows', axis=0, tiled=True)  114 us
    psum x1, waiting for transfers between devices, body(): lax.psum(gram_right.astype(jnp.bfloat16), 'rows').astype(jnp.float32)  91.3 us
    all_gather x4, blocking collectives, body(): lax.all_gather(left_now, 'ckpt', axis=1, tiled=True)  86.5 us
    all_gather x2, blocking collectives, body(): jax.lax.all_gather(mat, 'rows')  35.8 us
  transfers between devices with their start and end apart: 14, of which 14 were waited for; matrix products, arithmetic and copies ran while one was open for 0% of the time, Pallas kernels for 0%

profile of v1, /device:TPU:1, one launch (start us, length us, event | category | flops | bytes accessed | tf_op | source)
XLA Modules:
  0.0 1268.7 jit_solution(13062007667497709708)
XLA Ops:
  7.3 54.2 %all-gather.23.cloned.1.call-done = bf16[1,14336,64]{1,2,0:T(8,128)(2,1)} async-done(((bf16[1,896,64]{1,2,0:T(8,128)(2,1)}), bf16[1,14336,64]{1,2,0:T(8,128)(2,1)}) %all-gather.23.cloned.1.call-update) | async-done | bytes 1835024 | tf_op jit(solution)/shard_map/all_gather | solution.py:47
  61.5 5.9 fusion.6
  67.6 17.8 %all-gather.1 = f32[1024,64]{1,0:T(8,128)S(1)} all-gather(f32[64,64]{1,0:T(8,128)S(1)} %fusion.55), channel_id=3, replica_groups=mesh['ckpt'=16,'rows'=16] {'rows'}, dimensions={0}, use_global_device_ids=true | all-gather | bytes 278528 | tf_op jit(solution)/shard_map/all_gather | solution.py:50
  85.6 5.8 cholesky.74
  92.8 4.9 custom-call.10
  105.4 86.3 %reduce-scatter.7.cloned.1.call-done = bf16[896,64]{1,0:T(8,128)(2,1)} async-done(((bf16[14336,64]{1,0:T(8,128)(2,1)}), bf16[896,64]{1,0:T(8,128)(2,1)}) %reduce-scatter.7.cloned.1.call-update) | async-done | bytes 114704
  193.1 57.9 %psum.77 = f32[64,64]{0,1:T(8,128)S(1)} all-reduce(f32[64,64]{0,1:T(8,128)S(1)} %fusion.56), channel_id=1, replica_groups=mesh['ckpt'=16,'rows'=16] {'rows'}, use_global_device_ids=true, to_apply=%region_4.7 | all-reduce | flops 4096 | bytes 32768 | tf_op jit(solution)/shard_map/psum | solution.py:61
  251.0 5.8 cholesky.85
  258.2 4.9 custom-call.11
  265.3 60.2 %all-gather.11.cloned.1.call-done = bf16[14336,64]{0,1:T(8,128)(2,1)} async-done(((bf16[896,64]{0,1:T(8,128)(2,1)}), bf16[14336,64]{0,1:T(8,128)(2,1)}) %all-gather.11.cloned.1.call-update) | async-done | bytes 1835024 | tf_op jit(solution)/shard_map/all_gather | solution.py:47
  325.6 6.0 fusion.3
  331.8 18.0 %all-gather.2 = f32[1024,64]{1,0:T(8,128)S(1)} all-gather(f32[64,64]{1,0:T(8,128)S(1)} %fusion.57), channel_id=4, replica_groups=mesh['ckpt'=16,'rows'=16] {'rows'}, dimensions={0}, use_global_device_ids=true | all-gather | bytes 278528 | tf_op jit(solution)/shard_map/all_gather | solution.py:50
  349.9 5.8 cholesky.96
  357.1 4.9 custom-call.12
  369.8 86.3 %reduce-scatter.9.cloned.1.call-done = bf16[896,64]{1,0:T(8,128)(2,1)} async-done(((bf16[14336,64]{1,0:T(8,128)(2,1)}), bf16[896,64]{1,0:T(8,128)(2,1)}) %reduce-scatter.9.cloned.1.call-update) | async-done | bytes 114704
  457.3 57.9 %psum.82 = f32[64,64]{0,1:T(8,128)S(1)} all-reduce(f32[64,64]{0,1:T(8,128)S(1)} %fusion.58), channel_id=1, replica_groups=mesh['ckpt'=16,'rows'=16] {'rows'}, use_global_device_ids=true, to_apply=%region_11.15 | all-reduce | flops 4096 | bytes 32768 | tf_op jit(solution)/shard_map/psum | solution.py:61
  515.3 5.8 cholesky.107
  529.6 52.0 %all-gather.13.cloned.1.call-done = bf16[896,1024]{0,1:T(8,128)(2,1)} async-done(((bf16[896,64]{0,1:T(8,128)(2,1)}), bf16[896,1024]{0,1:T(8,128)(2,1)}) %all-gather.13.cloned.1.call-update) | async-done | bytes 1835024 | tf_op jit(solution)/shard_map/all_gather | solution.py:72
  584.7 91.3 %all-reduce.10.cloned.1.call-done = bf16[1024,64]{1,0:T(8,128)(2,1)} async-done(((bf16[1024,64]{1,0:T(8,128)(2,1)}), bf16[1024,64]{1,0:T(8,128)(2,1)}) %all-reduce.10.cloned.1.call-update) | async-done | bytes 131088 | tf_op jit(solution)/shard_map/psum | solution.py:78
  678.1 21.6 %all_gather.54 = bf16[256,1024]{0,1:T(8,128)(2,1)S(1)} all-gather(bf16[256,64]{0,1:T(8,128)(2,1)S(1)} %fusion.24), channel_id=1, replica_groups=mesh['ckpt'=16,'rows'=16] {'ckpt'}, dimensions={1}, use_global_device_ids=true | all-gather | bytes 557056 | tf_op jit(solution)/shard_map/all_gather | solution.py:71
  700.7 18.5 %all-gather.15.cloned.1.call-done = bf16[896,1024]{0,1:T(8,128)(2,1)} async-done(((bf16[896,64]{0,1:T(8,128)(2,1)}), bf16[896,1024]{0,1:T(8,128)(2,1)}) %all-gather.15.cloned.1.call-update) | async-done | bytes 1835024 | tf_op jit(solution)/shard_map/all_gather | solution.py:72
  722.2 92.2 %all-reduce.18.cloned.1.call-done = (bf16[1024,64]{1,0:T(8,128)(2,1)}, bf16[1024,64]{1,0:T(8,128)(2,1)}) async-done(((bf16[1024,64]{1,0:T(8,128)(2,1)}, bf16[1024,64]{1,0:T(8,128)(2,1)}), (bf16[1024,64]{1,0:T(8,128)(2,1)}, bf16[1024,64]{1,0:T(8,128)(2,1)})) %all-reduce.18.cloned.1.call-update) | async-done | bytes 262160 | tf_op jit(solution)/shard_map/psum | solution.py:77
  816.9 21.6 %all_gather.55 = bf16[256,1024]{0,1:T(8,128)(2,1)S(1)} all-gather(bf16[256,64]{0,1:T(8,128)(2,1)S(1)} %fusion.25), channel_id=1, replica_groups=mesh['ckpt'=16,'rows'=16] {'ckpt'}, dimensions={1}, use_global_device_ids=true | all-gather | bytes 557056 | tf_op jit(solution)/shard_map/all_gather | solution.py:71
  839.5 18.3 %all-gather.17.cloned.1.call-done = bf16[896,1024]{0,1:T(8,128)(2,1)} async-done(((bf16[896,64]{0,1:T(8,128)(2,1)}), bf16[896,1024]{0,1:T(8,128)(2,1)}) %all-gather.17.cloned.1.call-update) | async-done | bytes 1835024 | tf_op jit(solution)/shard_map/all_gather | solution.py:72
  860.9 92.2 %all-reduce.16.cloned.1.call-done = (bf16[1024,64]{1,0:T(8,128)(2,1)}, bf16[1024,64]{1,0:T(8,128)(2,1)}) async-done(((bf16[1024,64]{1,0:T(8,128)(2,1)}, bf16[1024,64]{1,0:T(8,128)(2,1)}), (bf16[1024,64]{1,0:T(8,128)(2,1)}, bf16[1024,64]{1,0:T(8,128)(2,1)})) %all-reduce.16.cloned.1.call-update) | async-done | bytes 262160 | tf_op jit(solution)/shard_map/psum | solution.py:77
  955.5 21.6 %all_gather.56 = bf16[256,1024]{0,1:T(8,128)(2,1)S(1)} all-gather(bf16[256,64]{0,1:T(8,128)(2,1)S(1)} %fusion.26), channel_id=1, replica_groups=mesh['ckpt'=16,'rows'=16] {'ckpt'}, dimensions={1}, use_global_device_ids=true | all-gather | bytes 557056 | tf_op jit(solution)/shard_map/all_gather | solution.py:71
  978.1 18.3 %all-gather.19.cloned.1.call-done = bf16[896,1024]{0,1:T(8,128)(2,1)} async-done(((bf16[896,64]{0,1:T(8,128)(2,1)}), bf16[896,1024]{0,1:T(8,128)(2,1)}) %all-gather.19.cloned.1.call-update) | async-done | bytes 1835024 | tf_op jit(solution)/shard_map/all_gather | solution.py:72
  999.4 92.1 %all-reduce.14.cloned.1.call-done = (bf16[1024,64]{1,0:T(8,128)(2,1)}, bf16[1024,64]{1,0:T(8,128)(2,1)}) async-done(((bf16[1024,64]{1,0:T(8,128)(2,1)}, bf16[1024,64]{1,0:T(8,128)(2,1)}), (bf16[1024,64]{1,0:T(8,128)(2,1)}, bf16[1024,64]{1,0:T(8,128)(2,1)})) %all-reduce.14.cloned.1.call-update) | async-done | bytes 262160 | tf_op jit(solution)/shard_map/psum | solution.py:77
  1094.0 21.6 %all_gather.57 = bf16[256,1024]{0,1:T(8,128)(2,1)S(1)} all-gather(bf16[256,64]{0,1:T(8,128)(2,1)S(1)} %fusion.27), channel_id=1, replica_groups=mesh['ckpt'=16,'rows'=16] {'ckpt'}, dimensions={1}, use_global_device_ids=true | all-gather | bytes 557056 | tf_op jit(solution)/shard_map/all_gather | solution.py:71
  1116.6 18.3 %all-gather.21.cloned.1.call-done = bf16[896,1024]{0,1:T(8,128)(2,1)} async-done(((bf16[896,64]{0,1:T(8,128)(2,1)}), bf16[896,1024]{0,1:T(8,128)(2,1)}) %all-gather.21.cloned.1.call-update) | async-done | bytes 1835024 | tf_op jit(solution)/shard_map/all_gather | solution.py:95
  1138.2 98.1 %all-reduce.12.cloned.1.call-done = (bf16[1024,64]{1,0:T(8,128)(2,1)}, bf16[896,1024]{0,1:T(8,128)(2,1)}) async-done(((bf16[1024,64]{1,0:T(8,128)(2,1)}, bf16[896,1024]{0,1:T(8,128)(2,1)}), (bf16[1024,64]{1,0:T(8,128)(2,1)}, bf16[896,1024]{0,1:T(8,128)(2,1)})) %all-reduce.12.cloned.1.call-update) | async-done | bytes 1966096 | tf_op jit(solution)/shard_map/psum | solution.py:77
  1238.4 20.8 %all_gather.58 = bf16[256,1024]{0,1:T(8,128)(2,1)S(1)} all-gather(bf16[256,64]{0,1:T(8,128)(2,1)S(1)} %convolution_convert_fusion.11), channel_id=1, replica_groups=mesh['ckpt'=16,'rows'=16] {'ckpt'}, dimensions={1}, use_global_device_ids=true | all-gather | bytes 557056 | tf_op jit(solution)/shard_map/all_gather | solution.py:94
  (109 shorter events, 67.3 us)
Async XLA Ops:
  6.5 54.9 %all-gather.23.cloned.1.call-start = ((), (), s32[]{:S(2)}) async-start(), calls=%async_computation.9 | async-start | bytes 1949696 | tf_op jit(solution)/shard_map/all_gather | solution.py:47
  7.3 184.5 %reduce-scatter.7.cloned.1.call-start = ((), (), s32[]{:S(2)}) async-start(), calls=%async_computation.10 | async-start | bytes 3899392
  105.4 220.2 %all-gather.11.cloned.1.call-start = ((), (), s32[]{:S(2)}) async-start(), calls=%async_computation.2 | async-start | bytes 1949696 | tf_op jit(solution)/shard_map/all_gather | solution.py:47
  265.3 190.8 %reduce-scatter.9.cloned.1.call-start = ((), (), s32[]{:S(2)}) async-start(), calls=%async_computation.11 | async-start | bytes 3899392
  369.7 212.0 %all-gather.13.cloned.1.call-start = ((), (), s32[]{:S(2)}) async-start(), calls=%async_computation.3 | async-start | bytes 1949696 | tf_op jit(solution)/shard_map/all_gather | solution.py:72
  529.6 146.4 %copy-start.7 = (bf16[896,64]{0,1:T(8,128)(2,1)S(1)}, bf16[896,64]{0,1:T(8,128)(2,1)}, u32[]{:S(2)}) copy-start(bf16[896,64]{0,1:T(8,128)(2,1)} %fusion.18) | copy-start | bytes 344068
  529.6 146.4 %all-reduce.10.cloned.1.call-start = ((), (), s32[]{:S(2)}) async-start(), calls=%async_computation.4 | async-start | bytes 524288 | tf_op jit(solution)/shard_map/psum | solution.py:78
  581.7 94.3 %copy-start.3 = (bf16[896,1024]{0,1:T(8,128)(2,1)S(1)}, bf16[896,1024]{0,1:T(8,128)(2,1)}, u32[]{:S(2)}) copy-start(bf16[896,1024]{0,1:T(8,128)(2,1)} %all-gather.13.cloned.1.call-done) | copy-start | bytes 5505028
  584.7 134.5 %all-gather.15.cloned.1.call-start = ((), (), s32[]{:S(2)}) async-start(), calls=%async_computation.5 | async-start | bytes 1949696 | tf_op jit(solution)/shard_map/all_gather | solution.py:72
  678.0 136.4 %all-reduce.18.cloned.1.call-start = ((), (), s32[]{:S(2)}) async-start(), calls=%async_computation.15 | async-start | bytes 1048576 | tf_op jit(solution)/shard_map/psum | solution.py:77
  699.7 114.7 %copy-start.6 = (bf16[896,64]{0,1:T(8,128)(2,1)S(1)}, bf16[896,64]{0,1:T(8,128)(2,1)}, u32[]{:S(2)}) copy-start(bf16[896,64]{0,1:T(8,128)(2,1)} %fusion.13) | copy-start | bytes 344068
  719.2 95.3 %copy-start.2 = (bf16[896,1024]{0,1:T(8,128)(2,1)S(1)}, bf16[896,1024]{0,1:T(8,128)(2,1)}, u32[]{:S(2)}) copy-start(bf16[896,1024]{0,1:T(8,128)(2,1)} %all-gather.15.cloned.1.call-done) | copy-start | bytes 5505028
  722.1 135.7 %all-gather.17.cloned.1.call-start = ((), (), s32[]{:S(2)}) async-start(), calls=%async_computation.6 | async-start | bytes 1949696 | tf_op jit(solution)/shard_map/all_gather | solution.py:72
  814.4 2.2 copy-start.9
  816.5 41.3 %copy-start.4 = (bf16[896,64]{0,1:T(8,128)(2,1)S(1)}, bf16[896,64]{0,1:T(8,128)(2,1)}, u32[]{:S(2)}) copy-start(bf16[896,64]{0,1:T(8,128)(2,1)} %fusion.14) | copy-start | bytes 344068
  816.6 136.5 %all-reduce.16.cloned.1.call-start = ((), (), s32[]{:S(2)}) async-start(), calls=%async_computation.14 | async-start | bytes 1048576 | tf_op jit(solution)/shard_map/psum | solution.py:77
  857.8 95.2 %copy-start = (bf16[896,1024]{0,1:T(8,128)(2,1)S(1)}, bf16[896,1024]{0,1:T(8,128)(2,1)}, u32[]{:S(2)}) copy-start(bf16[896,1024]{0,1:T(8,128)(2,1)} %all-gather.17.cloned.1.call-done) | copy-start | bytes 5505028
  860.8 135.6 %all-gather.19.cloned.1.call-start = ((), (), s32[]{:S(2)}) async-start(), calls=%async_computation.7 | async-start | bytes 1949696 | tf_op jit(solution)/shard_map/all_gather | solution.py:72
  953.0 2.2 copy-start.10
  955.1 41.3 %copy-start.5 = (bf16[896,64]{0,1:T(8,128)(2,1)S(1)}, bf16[896,64]{0,1:T(8,128)(2,1)}, u32[]{:S(2)}) copy-start(bf16[896,64]{0,1:T(8,128)(2,1)} %fusion.15) | copy-start | bytes 344068
  955.1 136.4 %all-reduce.14.cloned.1.call-start = ((), (), s32[]{:S(2)}) async-start(), calls=%async_computation.13 | async-start | bytes 1048576 | tf_op jit(solution)/shard_map/psum | solution.py:77
  996.4 95.1 %copy-start.1 = (bf16[896,1024]{0,1:T(8,128)(2,1)S(1)}, bf16[896,1024]{0,1:T(8,128)(2,1)}, u32[]{:S(2)}) copy-start(bf16[896,1024]{0,1:T(8,128)(2,1)} %all-gather.19.cloned.1.call-done) | copy-start | bytes 5505028
  999.4 135.5 %all-gather.21.cloned.1.call-start = ((), (), s32[]{:S(2)}) async-start(), calls=%async_computation.8 | async-start | bytes 1949696 | tf_op jit(solution)/shard_map/all_gather | solution.py:95
  1091.6 2.2 copy-start.8
  1093.7 142.7 %all-reduce.12.cloned.1.call-start = ((), (), s32[]{:S(2)}) async-start(), calls=%async_computation.12 | async-start | bytes 4194304 | tf_op jit(solution)/shard_map/psum | solution.py:77
  1136.3 0.7 copy-start.11
Sparse Core Ops, SparseCore 0:
  9.8 51.6 all-gather.22
  105.5 86.2 reduce-scatter.6
  265.4 60.1 all-gather.10
  369.8 86.1 reduce-scatter.8
  529.7 51.9 all-gather.12
  584.8 91.1 all-reduce.9
  678.2 40.9 all-gather.14
  722.4 92.0 all-reduce.17
  816.7 41.0 all-gather.16
  860.9 92.0 all-reduce.15
  955.3 41.0 all-gather.18
  999.5 91.9 all-reduce.13
  1093.8 41.1 all-gather.20
  1138.2 98.1 all-reduce.11
